TPU v7x, 128 devices: a whole 4x4x4 slice. The times are simulated.
128 devices in a mesh: shaft: 16 (over y, z), lat: 8 (over x, core).
Axes of the slice: x: 4, y: 4, z: 4, core: 2. Of those that a mesh axis runs over, the one named last changes fastest.
Arguments:
- sphere_position: float32 [3, 16, 16, 8, 128], P(None, 'shaft', 'lat'), may hold values from 0 to 5
- sphere_velocity: float32 [3, 16, 16, 8, 128], P(None, 'shaft', 'lat'), may hold values from -6 to 6
- sphere_radius: float32 [16, 16, 8, 128], P('shaft', 'lat'), may hold values from 0.4 to 0.6
- sphere_offset: float32 [3, 16, 16, 8, 128], P(None, 'shaft', 'lat'), may hold values from -6 to 6
- sphere_piece: int32 [16, 8, 2048], P('shaft', 'lat'), may hold values from 0 to 511, never falling along the last dimension, each value on 1 to 64 neighbouring positions
- piece_route: int32 [16, 8, 512], P('shaft', 'lat'), may hold values from 0 to 8, as said below
- piece_clump: int32 [16, 8, 512], P('shaft', 'lat'), may hold values from 0 to 255
- blade_phase: int32 [1], replicated, may hold values from 0 to 63
- clump_centre: float32 [3, 16, 8, 256], P(None, 'shaft', 'lat'), may hold values from -6 to 6
- clump_motion: float32 [6, 16, 8, 256], P(None, 'shaft', 'lat'), may hold values from -6 to 6
- clump_angles: float32 [3, 16, 8, 256], P(None, 'shaft', 'lat'), may hold values from -3.140625 to 3.140625
- clump_inverse_mass: float32 [16, 8, 256], P('shaft', 'lat'), may hold values from 0.05 to 0.5
- clump_inverse_inertia: float32 [3, 16, 8, 256], P(None, 'shaft', 'lat'), may hold values from 0.01 to 0.1
Outputs:
- clump_next: float32 [9, 16, 8, 256], P(None, 'shaft', 'lat')
- sphere_next: float32 [6, 16, 16, 8, 128], P(None, 'shaft', 'lat')
Inputs may be any that keep to these rules, and one draw needn't show every extreme that they name: `sphere_piece`: each device's spheres, in the order of the steps, form 512 runs of consecutive spheres numbered in order, each of 1 to 64 spheres; some run has exactly 64. `piece_route`: a code never names a lateral index outside the slabs; on every device no code is named by more than 128 pieces, and one code exactly 128 times.
All inputs are finite; a program needn't handle non-finite values.
Results may differ from a plain program's by a relative error of at most 0.0003.
Values sent between devices are 32-bit elements; how exact they have to be, the bound alone decides.
A program may use at most 128 MiB of HBM per device.

v0:
```python
import functools
import math

import jax
import jax.numpy as jnp
from jax import lax
from jax.experimental import pallas as pl
from jax.experimental.pallas import tpu as pltpu
from jax.sharding import PartitionSpec as P

PHASES = 64
CELL_SIDE = 5.0
BLADE_STIFFNESS = 20.0
BLADE_THICKNESS = 1.0
TIME_STEP = 0.5
GRAVITY = 0.5

REACH = 0.6001
CHUNK = 64
F32 = jnp.float32
BF16 = jnp.bfloat16
MESH = pl.DeviceIdType.MESH
LANES = (((1,), (1,)), ((), ()))
ROWS = (((1,), (0,)), ((), ()))
VMEM = pl.BlockSpec(memory_space=pltpu.VMEM)
SMEM = pl.BlockSpec(memory_space=pltpu.SMEM)
HBM = pl.BlockSpec(memory_space=pltpu.HBM)


def split3(x):
    high = x.astype(BF16)
    rest = x - high.astype(F32)
    middle = rest.astype(BF16)
    low = (rest - middle.astype(F32)).astype(BF16)
    return high, middle, low


def rows3(x):
    high = x.astype(BF16).astype(F32)
    rest = x - high
    middle = rest.astype(BF16).astype(F32)
    return jnp.concatenate([high, middle, rest - middle], 0)


def sum3(x):
    return x[0:8] + x[8:16] + x[16:24]


def one_hot(rows, row):
    length = row.shape[-1]
    ids = lax.broadcasted_iota(jnp.int32, (rows, length), 0)
    return jnp.where(ids == row, 1.0, 0.0).astype(BF16)


class Place:
    def __init__(self, n_shaft, n_lat):
        self.n_shaft, self.n_lat = n_shaft, n_lat
        self.s, self.l = lax.axis_index("shaft"), lax.axis_index("lat")

    def at(self, ds, dl):
        return {"shaft": lax.rem(self.s + ds + self.n_shaft, self.n_shaft), "lat": self.l + dl}

    def lateral(self, act):
        act(0)
        pl.when(self.l > 0)(lambda: act(-1))
        pl.when(self.l < self.n_lat - 1)(lambda: act(1))

    def greet(self):
        sem = pltpu.get_barrier_semaphore()

        def signal(dl):
            for ds in (-1, 0, 1):
                if (ds, dl) != (0, 0):
                    pl.semaphore_signal(
                        sem, inc=1, device_id=self.at(ds, dl), device_id_type=MESH
                    )

        self.lateral(signal)

    def meet(self):
        sem = pltpu.get_barrier_semaphore()
        edge = jnp.logical_or(self.l == 0, self.l == self.n_lat - 1)
        pl.semaphore_wait(sem, jnp.where(edge, 5, 8))


def halo_kernel(
    n_shaft,
    n_lat,
    pos,
    vel,
    rad,
    piece_hbm,
    route_hbm,
    clump_hbm,
    ext,
    hot_piece,
    hot_clump,
    route_rows,
    inside,
    tables,
    piece,
    route,
    clump,
    send_sem,
    recv_sem,
    own_sem,
    load_sem,
):
    place = Place(n_shaft, n_lat)

    def parts(j, si, lj):
        return (
            (pos.at[:, 0, j], ext.at[si, lj, 0:3]),
            (vel.at[:, 0, j], ext.at[si, lj, 3:6]),
            (rad.at[0, pl.ds(j, 1)], ext.at[si, lj, 6:7]),
        )

    def remote(j, ds, dl, si, lj):
        return [
            pltpu.make_async_remote_copy(
                src_ref=src,
                dst_ref=dst,
                send_sem=send_sem.at[si, lj, t],
                recv_sem=recv_sem.at[si, lj, t],
                device_id=place.at(ds, dl),
                device_id_type=MESH,
            )
            for t, (src, dst) in enumerate(parts(j, si, lj))
        ]

    def outgoing(dl):
        found = []
        for ds in (-1, 0, 1):
            for j in (0, 1):
                lj = j - 2 * dl + 1
                if 0 <= lj <= 3 and (ds, dl) != (0, 0):
                    found += remote(j, ds, dl, 1 - ds, lj)
        return found

    def incoming(dl):
        found = []
        for ds in (-1, 0, 1):
            for lj in {0: (1, 2), -1: (0,), 1: (3,)}[dl]:
                if (ds, dl) != (0, 0):
                    found += remote(0, ds, dl, 1 + ds, lj)
        return found

    own = [
        pltpu.make_async_copy(src, dst, own_sem.at[j, t])
        for j in (0, 1)
        for t, (src, dst) in enumerate(parts(j, 1, 1 + j))
    ]
    own += [
        pltpu.make_async_copy(src, dst, load_sem.at[t])
        for t, (src, dst) in enumerate(
            ((piece_hbm, piece), (route_hbm, route), (clump_hbm, clump))
        )
    ]
    for c in own:
        c.start()
    place.greet()
    place.meet()
    place.lateral(lambda dl: [c.start() for c in outgoing(dl)] and None)
    ext[:, :, 7] = jnp.zeros((3, 4, 8, 128), F32)

    @pl.when(place.l == 0)
    def _():
        ext[:, 0, 0:7] = jnp.zeros((3, 7, 8, 128), F32)

    @pl.when(place.l == n_lat - 1)
    def _():
        ext[:, 3, 0:7] = jnp.zeros((3, 7, 8, 128), F32)

    for c in own:
        c.wait()
    sub = lax.broadcasted_iota(jnp.int32, (8, 128), 0)
    every = one_hot(128, lax.broadcasted_iota(jnp.int32, (1, 128), 1))
    inside[...] = jnp.zeros((128, 128), F32)

    def cell(m):
        j, k = m // 8, m % 8
        mine = [ext[1, 1 + j, t, pl.ds(k, 1), :] for t in range(7)]
        mine[2] = mine[2] + (CELL_SIDE * k.astype(F32) - 20.0)
        own_table(mine, sub, tables.at[m])
        value = jnp.concatenate(mine + [mine[6]], 0)
        rows = lax.dot_general(every, keyed(value, sub), LANES, preferred_element_type=F32)
        zero = jnp.zeros((8, 128), F32)
        acc = (zero, zero, zero)
        for i in range(0, 128, CHUNK):
            acc = add_pairs(rows[i : i + CHUNK], tables.at[m], acc)
        for t in range(3):
            inside[pl.ds((j * 8 + t) * 8 + k, 1), :] = jnp.sum(acc[t], 0, keepdims=True)

    def cells(i, _):
        cell(2 * i)
        cell(2 * i + 1)
        return 0

    lax.fori_loop(0, 8, cells, 0)
    for m in range(16):
        hot_piece[:, m * 128 : m * 128 + 128] = one_hot(
            hot_piece.shape[0], piece[0, :, m * 128 : m * 128 + 128]
        )
    hot_clump[...] = one_hot(hot_clump.shape[0], clump[0])
    route_rows[...] = jnp.broadcast_to(route[0], route_rows.shape)
    place.lateral(lambda dl: [c.wait_recv() for c in incoming(dl)] and None)
    place.lateral(lambda dl: [c.wait_send() for c in outgoing(dl)] and None)


USUAL = {0: (128, 64, 64, 64), 1: (64, 24, 40, 24), 2: (32, 16, 24, 16)}
KEYS = 32
TERMS = 9


def kind(c):
    return (c // 3 != 1) + (c % 3 != 1)


def keyed(value, sub):
    radius = value[6:7]
    value = jnp.where(sub == 7, radius * radius * 0.0625, value)
    high = value.astype(BF16).astype(F32)
    rest = value - high
    middle = rest.astype(BF16).astype(F32)
    more = jnp.where(
        sub < 3,
        1.0,
        jnp.where(sub < 5, high[6:7], jnp.where(sub == 5, middle[6:7], 0.0)),
    )
    return jnp.concatenate([high, middle, rest - middle, more], 0).astype(BF16)


def own_table(own, sub, table):
    zero = jnp.zeros((8, 128), F32)

    def split(row):
        return [p.astype(F32) for p in split3(jnp.broadcast_to(row, (8, 128)))]

    def constants(row):
        high, middle, low = split(row)
        return jnp.where(sub == 0, high, jnp.where(sub == 1, middle, jnp.where(sub == 2, low, 0.0)))

    def put(t, same, more):
        block = jnp.concatenate([same, same, same, more], 0)
        table[:, t * 128 : t * 128 + 128] = block.astype(BF16)

    for t in range(7):
        put(t, jnp.where(sub == t, 1.0 if t == 6 else -1.0, zero), constants(own[t]))
    high, middle, low = split(4.0 * own[6])
    same = jnp.where(sub == 6, high, 0.0)
    more = jnp.where(sub == 4, low, jnp.where((sub == 3) | (sub == 5), middle, 0.0))
    put(7, same, more)
    put(
        8,
        jnp.where(sub == 7, 1.0, same * 0.03125),
        more * 0.03125 + constants(own[6] * own[6] * 0.0625),
    )


def pair_sums(pair, acc):
    dx, dy, dz, du, dv, dw, radii, product, least = pair
    square = dx * dx + dy * dy + dz * dz
    clamped = jnp.maximum(square, least)
    inverse = lax.rsqrt(clamped)
    delta = jnp.maximum(radii - clamped * inverse, 0.0)
    normal_speed = (du * dx + dv * dy + dw * dz) * inverse
    speed = du * du + dv * dv + dw * dw
    unit = square * (inverse * inverse)
    sliding = speed + normal_speed * normal_speed * (unit - 2.0)
    load = product * delta
    root = load * lax.rsqrt(jnp.maximum(load * radii, 1e-30))
    root2 = root * root
    cap = 2.5 * delta
    shear = root2 * cap * lax.rsqrt(jnp.maximum(root2 * (sliding + cap * cap), 0.0) + 1e-06)
    push = root * (cap + cap - normal_speed - 0.25)
    along = (push + shear * normal_speed) * inverse
    return (
        acc[0] + (along * dx - shear * du),
        acc[1] + (along * dy - shear * dv),
        acc[2] + (along * dz - shear * dw),
    )


def add_pairs(rows, table, acc):
    pairs = lax.dot_general(rows.astype(BF16), table[...], ROWS, preferred_element_type=F32)
    for g in range(0, rows.shape[0], 8):
        acc = pair_sums([pairs[g : g + 8, t * 128 : t * 128 + 128] for t in range(TERMS)], acc)
    return acc


def contact_kernel(
    lat_cells,
    phase,
    ext,
    inside,
    tables,
    off_hbm,
    angles_hbm,
    inertia_hbm,
    force,
    turning,
    off,
    angles,
    inertia,
    dest,
    count_v,
    count_s,
    bounds,
    picked,
    packed,
    copy_sem,
):
    loads = [
        pltpu.make_async_copy(src, dst, copy_sem.at[1 + t])
        for t, (src, dst) in enumerate(
            ((angles_hbm, angles), (inertia_hbm, inertia), (off_hbm, off))
        )
    ]
    for load in loads:
        load.start()
    sub = lax.broadcasted_iota(jnp.int32, (8, 128), 0)

    before = jnp.where(
        lax.broadcasted_iota(jnp.int32, (128, 128), 0)
        < lax.broadcasted_iota(jnp.int32, (128, 128), 1),
        1.0,
        0.0,
    ).astype(BF16)
    ones = jnp.ones((128, 128), BF16)
    for j in range(2):
        masks = []
        for c in range(9):
            di, dj = c // 3 - 1, c % 3 - 1
            base = ((1 + di) * 4 + 1 + j + dj) * 64
            x, y, z = (ext[base + 8 * t : base + 8 * t + 8, :] for t in range(3))
            radius = ext[base + 48 : base + 56, :]
            keep = radius > 0.0
            near = radius + REACH
            away = [v if d > 0 else CELL_SIDE - v for v, d in ((x, di), (y, dj)) if d]
            if len(away) == 1:
                keep &= away[0] < near
            if len(away) == 2:
                keep &= away[0] * away[0] + away[1] * away[1] < near * near
            low, high = z < near, CELL_SIDE - z < near
            kept = jnp.where(keep, 1.0, 0.0)
            low_f = jnp.where(low, kept, 0.0)
            high_f = jnp.where(high, kept, 0.0)
            mid_f = jnp.zeros((8, 128), F32) if c == 4 else kept - low_f - high_f
            masks += [low_f, mid_f, high_f]
        mask = jnp.concatenate(masks, 0).astype(BF16)
        prefix = lax.dot_general(mask, before, ROWS, preferred_element_type=F32)
        total = lax.dot_general(mask, ones, ROWS, preferred_element_type=F32)
        counts = lax.dot_general(ones[0:8], mask, LANES, preferred_element_type=F32)
        count_v[0:8, j * 256 : j * 256 + 216] = counts.astype(jnp.int32)
        over = jnp.full((8, 128), -1.0, F32)
        for c in range(9):
            a = c * 24
            low_p, mid_p, high_p = (prefix[a + 8 * t : a + 8 * t + 8] for t in range(3))
            low_n, mid_n, high_n = (total[a + 8 * t : a + 8 * t + 8] for t in range(3))
            spot = (
                masks[3 * c] * low_p
                + masks[3 * c + 1] * (low_n + mid_p)
                + masks[3 * c + 2] * (low_n + mid_n + high_p)
            )
            any_of = masks[3 * c] + masks[3 * c + 1] + masks[3 * c + 2]
            spot = jnp.where(any_of > 0.0, spot, -1.0).astype(jnp.int32)
            dest[(j * 9 + c) * 8 : (j * 9 + c) * 8 + 8, :] = spot
            sizes = (low_n + mid_n + high_n, low_n, mid_n, high_n)
            for size, usual in zip(sizes, USUAL[kind(c)]):
                over = jnp.maximum(over, size - usual)
        over = jnp.broadcast_to(jnp.max(over, 0, keepdims=True), (8, 128))
        count_v[8:16, j * 128 : j * 128 + 128] = over.astype(jnp.int32)
    copy = pltpu.make_async_copy(count_v, count_s, copy_sem.at[0])
    copy.start()

    angle = jnp.full((8, 128), phase[0].astype(F32) * (2.0 * math.pi / PHASES), F32)
    cos_b, sin_b = jnp.cos(angle), jnp.sin(angle)
    height_cells = 8
    centre_y, centre_z = 0.5 * CELL_SIDE * lat_cells, 0.5 * CELL_SIDE * height_cells
    reach = 0.45 * CELL_SIDE * min(lat_cells, height_cells)
    shaft_id = lax.axis_index("shaft").astype(F32)
    lat_id = (lax.axis_index("lat") * 2).astype(F32)
    up_id = sub.astype(F32)
    blade = []
    for j in range(2):
        base = (5 + j) * 64
        x, y, z = (ext[base + 8 * t : base + 8 * t + 8, :] for t in range(3))
        radius = ext[base + 48 : base + 56, :]
        x = CELL_SIDE * shaft_id + x
        y = CELL_SIDE * (lat_id + j) + y - centre_y
        z = CELL_SIDE * up_id + z - centre_z
        across = y * cos_b + z * sin_b
        radial = z * cos_b - y * sin_b
        depth = jnp.maximum(jnp.minimum(radius - across, radius + BLADE_THICKNESS + across), 0.0)
        window = jnp.maximum(radial * (reach - radial), 0.0) * (4.0 / (reach * reach))
        gate = jnp.maximum(jnp.cos(x * (2.0 * math.pi / (2.0 * CELL_SIDE))), 0.0)
        size = BLADE_STIFFNESS * depth * window * gate
        blade.append(size)

    loads[0].wait()
    loads[1].wait()
    n_clump = turning.shape[-1]
    cos_z, cos_y, cos_x = (jnp.cos(angles[t, 0]) for t in range(3))
    sin_z, sin_y, sin_x = (jnp.sin(angles[t, 0]) for t in range(3))
    rotation = [
        [
            cos_z * cos_y,
            cos_z * sin_y * sin_x - sin_z * cos_x,
            cos_z * sin_y * cos_x + sin_z * sin_x,
        ],
        [
            sin_z * cos_y,
            sin_z * sin_y * sin_x + cos_z * cos_x,
            sin_z * sin_y * cos_x - cos_z * sin_x,
        ],
        [-sin_y, cos_y * sin_x, cos_y * cos_x],
    ]
    for t, (a, b) in enumerate(((0, 0), (0, 1), (0, 2), (1, 1), (1, 2), (2, 2))):
        turning[t : t + 1, :] = TIME_STEP * sum(
            rotation[a][i] * inertia[i, 0] * rotation[b][i] for i in range(3)
        )
    turning[6:8, :] = jnp.zeros((2, n_clump), F32)
    lane = lax.broadcasted_iota(jnp.int32, (32, 128), 1)
    inert = jnp.where((lane >= 24) & (lane < 27), 1.0, 0.0)
    for j in range(2):

        def count(c, t, k):
            return count_s[0, j * 256 + (c * 3 + t) * 8 + k]

        def pick(c, k, rows, into):
            di, dj = c // 3 - 1, c % 3 - 1
            base = ((1 + di) * 4 + 1 + j + dj) * 64
            rise = CELL_SIDE * k.astype(F32) - 20.0
            shift = jnp.where(
                sub == 0,
                CELL_SIDE * di,
                jnp.where(sub == 1, CELL_SIDE * dj, jnp.where(sub == 2, rise, 0.0)),
            )
            value = ext[pl.ds(base + k, 8, stride=8), :] + shift
            spot = dest[pl.ds((j * 9 + c) * 8 + k, 1), :]
            keys = jnp.concatenate([keyed(value, sub), jnp.zeros((128 - KEYS, 128), BF16)], 0)
            into[k, 0:rows, :] = lax.dot_general(
                one_hot(rows, spot), keys, LANES, preferred_element_type=F32
            )

        sides = [c for c in range(9) if c != 4]

        def pick_some(i, _):
            for k in (4 * i, 4 * i + 1, 4 * i + 2, 4 * i + 3):
                for c in range(9):
                    pick(c, k, USUAL[kind(c)][0], picked.at[c])
            return 0

        lax.fori_loop(0, 2, pick_some, 0)
        if j == 0:
            copy.wait()

        def gather_level(k, offset, sizes):
            for t in range(3):
                start_of_part = offset
                if t == 2:
                    bounds[0, k] = offset
                for c in sides:
                    start = 0 if t == 0 else count(c, 0, k)
                    if t == 2:
                        start = start + count(c, 1, k)
                    length = sizes[kind(c)][1 + t]
                    packed[pl.ds(offset, length), :] = picked[c, k, pl.ds(start, length), :]
                    offset = offset + count(c, t, k)
                if t == 0:
                    bounds[1, k] = offset
                if t == 1:
                    packed[pl.ds(offset, 32), :] = inert
                    offset = jnp.maximum(offset, start_of_part + 32)
                    below, above = (k + 7) % 8, (k + 1) % 8
                    length = sizes[0][1]
                    start = count(4, 0, below)
                    packed[pl.ds(offset, length), :] = picked[4, below, pl.ds(start, length), :]
                    offset = offset + jnp.where(k > 0, count(4, 2, below), 0)
                    packed[pl.ds(offset, length), :] = picked[4, above, pl.ds(0, length), :]
                    offset = offset + jnp.where(k < 7, count(4, 0, above), 0)
                    packed[pl.ds(offset, 8), :] = inert[0:8]
                    offset = (offset + 7) // 8 * 8
            return offset

        def gather_usual():
            offset = 0
            for k in range(8):
                offset = gather_level(k, offset, USUAL)
            return offset

        def gather_any():
            def level(k, offset):
                for c in sides:
                    pick(c, k, 128, picked.at[c])
                return gather_level(k, offset, {t: (128,) * 4 for t in range(3)})

            return lax.fori_loop(0, 8, level, jnp.int32(0))

        end = lax.cond(count_s[8, j * 128] > 0, gather_any, gather_usual)
        packed[pl.ds(end, 32), :] = inert
        bounds[1, 8] = end

        def cell(k, _):
            first = jnp.where(k == 0, 0, bounds[0, jnp.maximum(k - 1, 0)])
            last = bounds[1, k + 1]
            table = tables.at[j * 8 + k]

            parts = (last - first + 31) // 32
            sums = (jnp.zeros((8, 128), F32),) * 3
            for size, times in ((128, parts // 4), (64, parts % 4 // 2), (32, parts % 2 // 1)):

                def chunk(i, acc, size=size):
                    at = pl.multiple_of(first + i * size, 8)
                    return add_pairs(packed[pl.ds(at, size), 0:KEYS], table, acc)

                sums = lax.fori_loop(0, times, chunk, sums)
                first = first + times * size
            for t in range(3):
                force[pl.ds((j * 8 + t) * 8 + k, 1), :] = jnp.sum(sums[t], 0, keepdims=True)
            return 0

        lax.fori_loop(0, 8, cell, 0)

    loads[2].wait()
    for j in range(2):
        fx, fy, fz = (
            force[(j * 8 + t) * 8 : (j * 8 + t) * 8 + 8, :]
            + inside[(j * 8 + t) * 8 : (j * 8 + t) * 8 + 8, :]
            for t in range(3)
        )
        fy, fz = fy + blade[j] * cos_b, fz + blade[j] * sin_b
        ox, oy, oz = (off[t, 0, j] for t in range(3))
        six = [fx, fy, fz, oy * fz - oz * fy, oz * fx - ox * fz, ox * fy - oy * fx]
        for t in range(8):
            force[(j * 8 + t) * 8 : (j * 8 + t) * 8 + 8, :] = (
                six[t] if t < 6 else jnp.zeros((8, 128), F32)
            )


def exchange_kernel(
    n_shaft,
    n_lat,
    force,
    hot_piece,
    hot_clump,
    route_rows,
    turning,
    motion_hbm,
    inverse_mass_hbm,
    table,
    motion,
    inverse_mass,
    part,
    got,
    send_sem,
    recv_sem,
    load_sem,
):
    place = Place(n_shaft, n_lat)
    n_clump = turning.shape[-1]
    place.greet()
    loads = [
        pltpu.make_async_copy(motion_hbm, motion, load_sem.at[0]),
        pltpu.make_async_copy(inverse_mass_hbm, inverse_mass, load_sem.at[1]),
    ]
    for load in loads:
        load.start()

    def sums_copy(ds, dl, slot):
        c = (ds + 1) * 3 + dl + 1
        return pltpu.make_async_remote_copy(
            src_ref=part.at[c],
            dst_ref=got.at[slot],
            send_sem=send_sem.at[0, slot],
            recv_sem=recv_sem.at[0, slot],
            device_id=place.at(ds, dl),
            device_id_type=MESH,
        )

    def table_copy(ds, dl, slot):
        return pltpu.make_async_remote_copy(
            src_ref=table.at[4],
            dst_ref=table.at[slot],
            send_sem=send_sem.at[1, slot],
            recv_sem=recv_sem.at[1, slot],
            device_id=place.at(ds, dl),
            device_id_type=MESH,
        )

    def around(act, dl):
        for ds in (-1, 0, 1):
            if (ds, dl) != (0, 0):
                act(ds, dl)

    terms = [
        rows3(force[pl.ds(j * 64 + k, 8, stride=8), :]).astype(BF16) for j in range(2) for k in range(8)
    ]
    sums = lax.dot_general(
        jnp.concatenate(terms, 1), hot_piece[...], LANES, preferred_element_type=F32
    )
    sums = rows3(sum3(sums))
    route = jnp.concatenate([route_rows[...]] * 3, 0)
    routed = jnp.concatenate([jnp.where(route == c, sums, 0.0) for c in range(9)], 0)
    sums = lax.dot_general(
        routed.astype(BF16), hot_clump[...], LANES, preferred_element_type=F32
    )
    for c in range(9):
        part[c] = sum3(sums[24 * c : 24 * c + 24])

    def clear(edge, column):
        @pl.when(place.l == edge)
        def _():
            for row in range(3):
                table[row * 3 + column] = jnp.zeros((8, n_clump), F32)
                got[row * 3 + 2 - column] = jnp.zeros((8, n_clump), F32)

    clear(0, 0)
    clear(n_lat - 1, 2)
    place.meet()
    place.lateral(
        lambda dl: around(lambda ds, d: sums_copy(ds, d, (ds + 1) * 3 + d + 1).start(), dl)
    )
    for load in loads:
        load.wait()
    place.lateral(
        lambda dl: around(lambda ds, d: sums_copy(ds, d, 8 - (ds + 1) * 3 - d - 1).wait_recv(), dl)
    )
    sums = part[4]
    for c in range(9):
        if c != 4:
            sums = sums + got[c]
    rows = []
    for t in range(3):
        pull = -GRAVITY if t == 2 else 0.0
        rows.append(motion[t, 0] + TIME_STEP * (inverse_mass[0] * sums[t : t + 1] + pull))
    torque = [sums[3 + t : 4 + t] for t in range(3)]
    order = ((0, 1, 2), (1, 3, 4), (2, 4, 5))
    for t in range(3):
        change = sum(turning[order[t][i] : order[t][i] + 1, :] * torque[i] for i in range(3))
        rows.append(motion[3 + t, 0] + change)
    table[4] = jnp.concatenate(rows + [jnp.zeros((2, n_clump), F32)], 0)
    place.lateral(
        lambda dl: around(lambda ds, d: table_copy(ds, d, 8 - (ds + 1) * 3 - d - 1).start(), dl)
    )
    place.lateral(
        lambda dl: around(lambda ds, d: table_copy(ds, d, (ds + 1) * 3 + d + 1).wait_recv(), dl)
    )
    place.lateral(
        lambda dl: around(lambda ds, d: sums_copy(ds, d, (ds + 1) * 3 + d + 1).wait_send(), dl)
    )
    place.lateral(
        lambda dl: around(lambda ds, d: table_copy(ds, d, 8 - (ds + 1) * 3 - d - 1).wait_send(), dl)
    )


def spread_kernel(
    table,
    hot_piece,
    hot_clump,
    route_rows,
    centre_hbm,
    off_hbm,
    clump_hbm,
    sphere_hbm,
    centre,
    off,
    clump_out,
    sphere_out,
    pose,
    sem,
):
    loads = [
        pltpu.make_async_copy(centre_hbm, centre, sem.at[0]),
        pltpu.make_async_copy(off_hbm, off, sem.at[1]),
    ]
    for load in loads:
        load.start()
    tables = jnp.concatenate([rows3(table[c]) for c in range(9)], 0).astype(BF16)
    found = lax.dot_general(tables, hot_clump[...], ROWS, preferred_element_type=F32)
    route = jnp.concatenate([route_rows[...]] * 3, 0)
    by_piece = found[0:24]
    for c in range(1, 9):
        by_piece = jnp.where(route == c, found[24 * c : 24 * c + 24], by_piece)
    by_sphere = sum3(
        lax.dot_general(by_piece.astype(BF16), hot_piece[...], ROWS, preferred_element_type=F32)
    )
    loads[0].wait()
    for t in range(6):
        row = table[4, t : t + 1, :]
        if t < 3:
            clump_out[t, 0] = centre[t, 0] + TIME_STEP * row
        clump_out[3 + t, 0] = row
    stores = [pltpu.make_async_copy(clump_out, clump_hbm, sem.at[2])]
    stores[0].start()
    for m in range(16):
        pose[m * 8 : m * 8 + 8, :] = by_sphere[:, m * 128 : m * 128 + 128]
    loads[1].wait()
    for j in range(2):
        vx, vy, vz, sx, sy, sz = (
            pose[pl.ds(j * 64 + t, 8, stride=8), :] for t in range(6)
        )
        bx, by, bz = (off[t, 0, j] for t in range(3))
        hx, hy, hz = (0.5 * TIME_STEP * s for s in (sx, sy, sz))
        scale = 2.0 / (1.0 + (hx * hx + hy * hy + hz * hz))
        cx, cy, cz = hy * bz - hz * by, hz * bx - hx * bz, hx * by - hy * bx
        tx = bx + scale * (cx + hy * cz - hz * cy)
        ty = by + scale * (cy + hz * cx - hx * cz)
        tz = bz + scale * (cz + hx * cy - hy * cx)
        sphere_out[0, 0, j], sphere_out[1, 0, j], sphere_out[2, 0, j] = tx, ty, tz
        sphere_out[3, 0, j] = vx + (sy * tz - sz * ty)
        sphere_out[4, 0, j] = vy + (sz * tx - sx * tz)
        sphere_out[5, 0, j] = vz + (sx * ty - sy * tx)
        stores.append(
            pltpu.make_async_copy(
                sphere_out.at[:, :, pl.ds(j, 1)], sphere_hbm.at[:, :, pl.ds(j, 1)], sem.at[3 + j]
            )
        )
        stores[-1].start()
    for store in stores:
        store.wait()


def contact_call(lat_cells, blade_phase, ext, inside, tables, off, angles, inertia, **extra):
    n_clump = angles.shape[-1]
    return pl.pallas_call(
        functools.partial(contact_kernel, lat_cells),
        out_shape=(
            jax.ShapeDtypeStruct((128, 128), F32),
            jax.ShapeDtypeStruct((8, n_clump), F32),
        ),
        in_specs=[SMEM] + [VMEM] * 3 + [HBM] * 3,
        out_specs=(VMEM, VMEM),
        scratch_shapes=[
            pltpu.VMEM(off.shape, F32),
            pltpu.VMEM(angles.shape, F32),
            pltpu.VMEM(inertia.shape, F32),
            pltpu.VMEM((144, 128), jnp.int32),
            pltpu.VMEM((16, 512), jnp.int32),
            pltpu.SMEM((16, 512), jnp.int32),
            pltpu.SMEM((2, 16), jnp.int32),
            pltpu.VMEM((9, 8, 256, 128), F32),
            pltpu.VMEM((9 * 1024 + 8 * 72 + 256, 128), F32),
            pltpu.SemaphoreType.DMA((4,)),
        ],
        compiler_params=pltpu.CompilerParams(vmem_limit_bytes=24 << 20),
        name="contact",
        **extra,
    )(blade_phase, ext, inside, tables, off, angles, inertia)


def on_device(
    n_shaft,
    n_lat,
    sphere_position,
    sphere_velocity,
    sphere_radius,
    sphere_offset,
    sphere_piece,
    piece_route,
    piece_clump,
    blade_phase,
    clump_centre,
    clump_motion,
    clump_angles,
    clump_inverse_mass,
    clump_inverse_inertia,
):
    n_piece, n_clump = piece_route.shape[-1], clump_angles.shape[-1]
    sphere_position, sphere_velocity, sphere_radius, sphere_piece, piece_route, piece_clump = (
        pltpu.with_memory_space_constraint(v, pltpu.HBM)
        for v in (
            sphere_position,
            sphere_velocity,
            sphere_radius,
            sphere_piece,
            piece_route,
            piece_clump,
        )
    )
    sphere_offset, clump_centre, clump_motion = (
        pltpu.with_memory_space_constraint(v, pltpu.HBM)
        for v in (sphere_offset, clump_centre, clump_motion)
    )
    clump_angles, clump_inverse_mass, clump_inverse_inertia = (
        pltpu.with_memory_space_constraint(v, pltpu.HBM)
        for v in (clump_angles, clump_inverse_mass, clump_inverse_inertia)
    )
    ext, hot_piece, hot_clump, route_rows, inside, tables = pl.pallas_call(
        functools.partial(halo_kernel, n_shaft, n_lat),
        out_shape=(
            jax.ShapeDtypeStruct((3, 4, 8, 8, 128), F32),
            jax.ShapeDtypeStruct((n_piece, 2048), BF16),
            jax.ShapeDtypeStruct((n_clump, n_piece), BF16),
            jax.ShapeDtypeStruct((8, n_piece), jnp.int32),
            jax.ShapeDtypeStruct((128, 128), F32),
            jax.ShapeDtypeStruct((16, KEYS, TERMS * 128), BF16),
        ),
        in_specs=[HBM] * 6,
        out_specs=(VMEM,) * 6,
        scratch_shapes=[
            pltpu.VMEM(sphere_piece.shape, jnp.int32),
            pltpu.VMEM(piece_route.shape, jnp.int32),
            pltpu.VMEM(piece_clump.shape, jnp.int32),
            pltpu.SemaphoreType.DMA((3, 4, 3)),
            pltpu.SemaphoreType.DMA((3, 4, 3)),
            pltpu.SemaphoreType.DMA((2, 3)),
            pltpu.SemaphoreType.DMA((3,)),
        ],
        compiler_params=pltpu.CompilerParams(
            collective_id=0, has_side_effects=True, vmem_limit_bytes=16 << 20
        ),
        name="halo",
    )(
        sphere_position,
        sphere_velocity,
        sphere_radius,
        sphere_piece,
        piece_route,
        piece_clump,
    )
    force, turning = contact_call(
        2 * n_lat,
        blade_phase,
        ext.reshape(768, 128),
        inside,
        tables,
        sphere_offset,
        clump_angles,
        clump_inverse_inertia,
    )
    table = pl.pallas_call(
        functools.partial(exchange_kernel, n_shaft, n_lat),
        out_shape=jax.ShapeDtypeStruct((9, 8, n_clump), F32),
        in_specs=[VMEM] * 5 + [HBM] * 2,
        out_specs=VMEM,
        scratch_shapes=[
            pltpu.VMEM(clump_motion.shape, F32),
            pltpu.VMEM(clump_inverse_mass.shape, F32),
            pltpu.VMEM((9, 8, n_clump), F32),
            pltpu.VMEM((9, 8, n_clump), F32),
            pltpu.SemaphoreType.DMA((2, 9)),
            pltpu.SemaphoreType.DMA((2, 9)),
            pltpu.SemaphoreType.DMA((2,)),
        ],
        compiler_params=pltpu.CompilerParams(
            collective_id=1, has_side_effects=True, vmem_limit_bytes=16 << 20
        ),
        name="exchange",
    )(force, hot_piece, hot_clump, route_rows, turning, clump_motion, clump_inverse_mass)
    return pl.pallas_call(
        spread_kernel,
        out_shape=(
            jax.ShapeDtypeStruct((9, 1, 1, n_clump), F32),
            jax.ShapeDtypeStruct((6, 1, 2, 8, 128), F32),
        ),
        in_specs=[VMEM] * 4 + [HBM] * 2,
        out_specs=(HBM, HBM),
        scratch_shapes=[
            pltpu.VMEM(clump_centre.shape, F32),
            pltpu.VMEM(sphere_offset.shape, F32),
            pltpu.VMEM((9, 1, 1, n_clump), F32),
            pltpu.VMEM((6, 1, 2, 8, 128), F32),
            pltpu.VMEM((128, 128), F32),
            pltpu.SemaphoreType.DMA((5,)),
        ],
        compiler_params=pltpu.CompilerParams(vmem_limit_bytes=16 << 20),
        name="spread",
    )(table, hot_piece, hot_clump, route_rows, clump_centre, sphere_offset)


def solution(mesh):
    placed = (
        P(None, "shaft", "lat", None, None),
        P(None, "shaft", "lat", None, None),
        P("shaft", "lat", None, None),
        P(None, "shaft", "lat", None, None),
        P("shaft", "lat", None),
        P("shaft", "lat", None),
        P("shaft", "lat", None),
        P(),
        P(None, "shaft", "lat", None),
        P(None, "shaft", "lat", None),
        P(None, "shaft", "lat", None),
        P("shaft", "lat", None),
        P(None, "shaft", "lat", None),
    )
    return jax.shard_map(
        functools.partial(on_device, mesh.shape["shaft"], mesh.shape["lat"]),
        mesh=mesh,
        in_specs=placed,
        out_specs=(P(None, "shaft", "lat", None), P(None, "shaft", "lat", None, None)),
        check_vma=False,
    )
```

profile of v0, /device:TPU:1, one launch (start us, length us, event | category | flops | bytes accessed | tf_op | source)
XLA Modules:
  0.0 50.4 jit_solution(10282172488738873916)
XLA Ops:
  1.3 16.2 %halo.1 = (f32[3,4,8,8,128]{4,3,2,1,0:T(8,128)S(1)}, bf16[512,2048]{1,0:T(8,128)(2,1)S(1)}, bf16[256,512]{1,0:T(8,128)(2,1)S(1)}, s32[8,512]{1,0:T(8,128)S(1)}, ...) custom-call(f32[3,1,2,8,128]{4,3,2,1,0:T(8,128)} %pos.1, f32[3,1,2,8,128]{4,3,2,1,0:T(8,128)} %vel.1, ...), custom_call_target="tpu_custom_call" | custom-call | tf_op jit(solution)/shard_map/halo/pallas_call | solution.py:789
  17.5 14.8 %contact.1 = (f32[128,128]{1,0:T(8,128)S(1)}, f32[8,256]{1,0:T(8,128)S(1)}) custom-call(s32[1]{0:T(128)S(6)} %copy.15.phase, f32[768,128]{1,0:T(8,128)S(1)} %bitcast.1, f32[128,128]{1,0:T(8,128)S(1)} %get-tuple-element.11.inside, bf16[16,32,1152]{2,1,0:T(8,128)(2,1)S(1)} %get-tuple-element.12.tables, f32[3,1,2,8,128]{4,3,2,1,0:T(8,128)} %off_hbm.3, ...), custom_call_target="tpu_custom_call" | custom-call | tf_op jit(solution)/shard_map/contact/pallas_call | solution.py:726
  32.3 16.1 %exchange.1.table = f32[9,8,256]{2,1,0:T(8,128)S(1)} custom-call(f32[128,128]{1,0:T(8,128)S(1)} %get-tuple-element.13.force, bf16[512,2048]{1,0:T(8,128)(2,1)S(1)} %get-tuple-element.14.hot_piece, bf16[256,512]{1,0:T(8,128)(2,1)S(1)} %get-tuple-element.15.hot_clump, s32[8,512]{1,0:T(8,128)S(1)} %get-tuple-element.16.route_rows, ...), custom_call_target="tpu_custom_call" | custom-call | tf_op jit(solution)/shard_map/exchange/pallas_call | solution.py:832
  48.5 2.0 %spread.1 = (f32[9,1,1,256]{3,2,1,0:T(1,128)}, f32[6,1,2,8,128]{4,3,2,1,0:T(8,128)}) custom-call(f32[9,8,256]{2,1,0:T(8,128)S(1)} %exchange.1.table, bf16[512,2048]{1,0:T(8,128)(2,1)S(1)} %get-tuple-element.14.hot_piece, bf16[256,512]{1,0:T(8,128)(2,1)S(1)} %get-tuple-element.15.hot_clump, s32[8,512]{1,0:T(8,128)S(1)} %get-tuple-element.16.route_rows, ...), custom_call_target="tpu_custom_call" | custom-call | tf_op jit(solution)/shard_map/spread/pallas_call | solution.py:851
where the time goes:
time: 51.3 us; the launch traced here: 50.4 us
  Pallas kernels  49.1 us (96%)
  between operations  1.3 us (3%)
    pallas_call x1, Pallas kernels, on_device(): pl.pallas_call(functools.partial(halo_kernel, n_shaft, n_lat), out_shape=...  16.2 us
    pallas_call x1, Pallas kernels, on_device(): pl.pallas_call(functools.partial(exchange_kernel, n_shaft, n_lat), out_sh...  16.1 us
    pallas_call x1, Pallas kernels, contact_call(): pl.pallas_call(functools.partial(contact_kernel, lat_cells), out_shape=(j...  14.8 us
    pallas_call x1, Pallas kernels, on_device(): pl.pallas_call(spread_kernel, out_shape=(jax.ShapeDtypeStruct((9, 1, 1, n...  1.96 us

commit v1 on v0

--- a/solution.py
+++ b/solution.py
@@ -48,8 +48,8 @@
 
 def one_hot(rows, row):
     length = row.shape[-1]
-    ids = lax.broadcasted_iota(jnp.int32, (rows, length), 0)
-    return jnp.where(ids == row, 1.0, 0.0).astype(BF16)
+    ids = lax.broadcasted_iota(jnp.int16, (rows, length), 0)
+    return jnp.where(ids == row.astype(jnp.int16), jnp.ones((), BF16), jnp.zeros((), BF16))
 
 
 class Place:
@@ -192,11 +192,11 @@
             inside[pl.ds((j * 8 + t) * 8 + k, 1), :] = jnp.sum(acc[t], 0, keepdims=True)
 
     def cells(i, _):
-        cell(2 * i)
-        cell(2 * i + 1)
+        for t in range(4):
+            cell(4 * i + t)
         return 0
 
-    lax.fori_loop(0, 8, cells, 0)
+    lax.fori_loop(0, 4, cells, 0)
     for m in range(16):
         hot_piece[:, m * 128 : m * 128 + 128] = one_hot(
             hot_piece.shape[0], piece[0, :, m * 128 : m * 128 + 128]

time: 51.3 us -> 51.9 us (1.012); the launches traced: 50.4 us -> 51.7 us
  Pallas kernels: 49.1 us -> 50.4 us
    pallas_call x1, Pallas kernels: 14.8 us -> 20.8 us  [contact_call(): pl.pallas_call(functools.partial(contact_kernel, lat_cells), out_shape=(j...]
    pallas_call x1, Pallas kernels: 16.1 us -> 12.6 us  [on_device(): pl.pallas_call(functools.partial(exchange_kernel, n_shaft, n_lat), out_sh...]
    pallas_call x1, Pallas kernels: 16.2 us -> 15 us  [on_device(): pl.pallas_call(functools.partial(halo_kernel, n_shaft, n_lat), out_shape=...]
where the time goes in v1:
time: 51.9 us; the launch traced here: 51.7 us
  Pallas kernels  50.4 us (97%)
  between operations  1.3 us (3%)
    pallas_call x1, Pallas kernels, contact_call(): pl.pallas_call(functools.partial(contact_kernel, lat_cells), out_shape=(j...  20.8 us
    pallas_call x1, Pallas kernels, on_device(): pl.pallas_call(functools.partial(halo_kernel, n_shaft, n_lat), out_shape=...  15 us
    pallas_call x1, Pallas kernels, on_device(): pl.pallas_call(functools.partial(exchange_kernel, n_shaft, n_lat), out_sh...  12.6 us
    pallas_call x1, Pallas kernels, on_device(): pl.pallas_call(spread_kernel, out_shape=(jax.ShapeDtypeStruct((9, 1, 1, n...  1.96 us

profile of v1, /device:TPU:1, one launch (start us, length us, event | category | flops | bytes accessed | tf_op | source)
XLA Modules:
  0.0 51.7 jit_solution(4072084894862954627)
XLA Ops:
  1.3 15.0 %halo.1 = (f32[3,4,8,8,128]{4,3,2,1,0:T(8,128)S(1)}, bf16[512,2048]{1,0:T(8,128)(2,1)S(1)}, bf16[256,512]{1,0:T(8,128)(2,1)S(1)}, s32[8,512]{1,0:T(8,128)S(1)}, ...) custom-call(f32[3,1,2,8,128]{4,3,2,1,0:T(8,128)} %pos.1, f32[3,1,2,8,128]{4,3,2,1,0:T(8,128)} %vel.1, ...), custom_call_target="tpu_custom_call" | custom-call | tf_op jit(solution)/shard_map/halo/pallas_call | solution.py:789
  16.3 20.8 %contact.1 = (f32[128,128]{1,0:T(8,128)S(1)}, f32[8,256]{1,0:T(8,128)S(1)}) custom-call(s32[1]{0:T(128)S(6)} %copy.15.phase, f32[768,128]{1,0:T(8,128)S(1)} %bitcast.1, f32[128,128]{1,0:T(8,128)S(1)} %get-tuple-element.11.inside, bf16[16,32,1152]{2,1,0:T(8,128)(2,1)S(1)} %get-tuple-element.12.tables, f32[3,1,2,8,128]{4,3,2,1,0:T(8,128)} %off_hbm.3, ...), custom_call_target="tpu_custom_call" | custom-call | tf_op jit(solution)/shard_map/contact/pallas_call | solution.py:726
  37.1 12.6 %exchange.1.table = f32[9,8,256]{2,1,0:T(8,128)S(1)} custom-call(f32[128,128]{1,0:T(8,128)S(1)} %get-tuple-element.13.force, bf16[512,2048]{1,0:T(8,128)(2,1)S(1)} %get-tuple-element.14.hot_piece, bf16[256,512]{1,0:T(8,128)(2,1)S(1)} %get-tuple-element.15.hot_clump, s32[8,512]{1,0:T(8,128)S(1)} %get-tuple-element.16.route_rows, ...), custom_call_target="tpu_custom_call" | custom-call | tf_op jit(solution)/shard_map/exchange/pallas_call | solution.py:832
  49.8 2.0 %spread.1 = (f32[9,1,1,256]{3,2,1,0:T(1,128)}, f32[6,1,2,8,128]{4,3,2,1,0:T(8,128)}) custom-call(f32[9,8,256]{2,1,0:T(8,128)S(1)} %exchange.1.table, bf16[512,2048]{1,0:T(8,128)(2,1)S(1)} %get-tuple-element.14.hot_piece, bf16[256,512]{1,0:T(8,128)(2,1)S(1)} %get-tuple-element.15.hot_clump, s32[8,512]{1,0:T(8,128)S(1)} %get-tuple-element.16.route_rows, ...), custom_call_target="tpu_custom_call" | custom-call | tf_op jit(solution)/shard_map/spread/pallas_call | solution.py:851
